TPU v7x, 32 devices: a whole 2x2x4 slice. The times are simulated.
32 devices in a mesh: band: 4 (over z), lev: 4 (over y, core), grp: 2 (over x).
Axes of the slice: x: 2, y: 2, z: 4, core: 2. Of those that a mesh axis runs over, the one named last changes fastest.
Arguments:
- fourier: bfloat16 [3, 8, 2, 2, 2, 48, 96], P(None, 'lev', None, None, 'grp', 'band'), may hold values from -6 to 6
- legendre: bfloat16 [96, 2, 48, 2, 48], P('band', None, 'lev', 'grp'), may hold values from -0.625 to 0.625
- lat_points: int32 [2, 48], P('grp', 'band'), may hold values from 20 to 400, as said below
- wave_slots: int32 [96], replicated, may hold values from 0 to 95, as said below
- vertical: float32 [8, 8], replicated, may hold values from -2 to 2
Outputs:
- spectral: bfloat16 [96, 2, 4, 8, 2, 48], P('band', None, None, None, None, ('lev', 'grp'))
Inputs may be any that keep to these rules, and one draw needn't show every extreme that they name: `lat_points`: the values are 20 + 4 i for i = 0 .. 95, each once (octahedral point counts of the latitude pairs, spread over devices). `wave_slots`: every wavenumber appears once; slots 2 i and 2 i + 1 hold wavenumbers m and 95 - m.
All inputs are finite; a program needn't handle non-finite values.
Results may differ from a plain program's by a relative error of at most 0.0053.
Values may be sent and summed in bfloat16 or wider, within the bound.
No kernel may reach another device: no remote copies, remote signals or barrier semaphores. Data moves between devices by JAX's collectives and lax.ppermute only.
A program may use at most 64 MiB of HBM per device.

v0:
```python
import jax
import jax.numpy as jnp
from jax import lax
from jax.sharding import PartitionSpec as P


def body(fourier, legendre, lat_points, wave_slots, vertical):
    wave_count = fourier.shape[6]
    cutoff = jnp.minimum(wave_count - 1, (lat_points - 1) // 2)
    wave_ids = lax.broadcasted_iota(jnp.int32, (1, 1, wave_count), 2)
    kept_mask = wave_ids <= cutoff[:, :, None]
    masked = jnp.where(kept_mask, fourier, jnp.zeros((), fourier.dtype))
    slot_table = (
        wave_slots[:, None] == lax.broadcasted_iota(jnp.int32, (wave_count, wave_count), 1)
    ).astype(jnp.bfloat16)
    ordered = lax.dot_general(
        slot_table, masked, (((1,), (6,)), ((), ())), preferred_element_type=jnp.float32
    ).astype(jnp.bfloat16)
    at_owners = lax.all_to_all(ordered, "band", split_axis=0, concat_axis=6, tiled=True)
    coeffs = lax.all_gather(at_owners, "lev", axis=2, tiled=True)
    level_count = coeffs.shape[2]
    level_rows = lax.broadcasted_iota(jnp.int32, (level_count, level_count), 0)
    level_cols = lax.broadcasted_iota(jnp.int32, (level_count, level_count), 1)
    integral = jnp.where(level_cols >= level_rows, vertical, jnp.zeros((), vertical.dtype))
    geopotential = jnp.einsum(
        "lk,skchgr->slchgr",
        integral,
        coeffs[:, 2].astype(jnp.float32),
        precision=lax.Precision.HIGHEST,
    ).astype(jnp.bfloat16)
    fields = jnp.concatenate([coeffs, geopotential[:, None]], axis=1)
    northern = fields[:, :, :, :, 0].astype(jnp.float32)
    southern = fields[:, :, :, :, 1].astype(jnp.float32)
    parity = jnp.stack(
        [(northern + southern).astype(jnp.bfloat16), (northern - southern).astype(jnp.bfloat16)],
        axis=4,
    )
    partial_value = lax.dot_general(
        parity, legendre, (((5, 6), (3, 4)), ((0, 4), (0, 1))), preferred_element_type=jnp.float32
    )
    summed = lax.psum_scatter(partial_value, "grp", scatter_dimension=5, tiled=True)
    slot_count = summed.shape[0]
    half_count = summed.shape[5]
    slot_waves = lax.dynamic_slice_in_dim(
        wave_slots, lax.axis_index("band") * slot_count, slot_count
    )
    block_start = (
        lax.axis_index("lev") * lax.axis_size("grp") + lax.axis_index("grp")
    ) * half_count
    half_ids = block_start + lax.broadcasted_iota(jnp.int32, (1, 1, half_count), 2)
    parity_ids = lax.broadcasted_iota(jnp.int32, (1, 2, 1), 1)
    total = slot_waves[:, None, None] + 2 * half_ids + parity_ids
    valid = (total <= wave_count - 1)[:, :, None, None, None, :]
    return jnp.where(valid, summed, 0.0).astype(jnp.bfloat16)


def solution(mesh):
    placed = (
        P(None, "lev", None, None, "grp", "band", None),
        P("band", None, "lev", "grp", None),
        P("grp", "band"),
        P(),
        P(),
    )
    return jax.shard_map(
        body,
        mesh=mesh,
        in_specs=placed,
        out_specs=P("band", None, None, None, None, ("lev", "grp")),
        check_vma=False,
    )
```

profile of v0, /device:TPU:0, one launch (start us, length us, event | category | flops | bytes accessed | tf_op | source)
XLA Modules:
  0.0 61.3 jit_solution(10844568631659761171)
XLA Ops:
  6.5 0.0 copy-start
  6.5 0.0 copy-start.2
  6.5 0.7 %minimum_bitcast_fusion = s32[12]{0:T(128)S(1)} fusion(s32[1,12]{1,0:T(1,128)} %param.7), kind=kLoop, calls=%fused_computation.34 | loop fusion | flops 204 | bytes 96 | tf_op jit(solution)/shard_map/le | solution.py:11
  7.3 0.1 iota_compare_fusion.1
  7.3 1.0 %fusion.9 = bf16[3,2,2,2,12,96]{5,3,4,2,1,0:T(2,128)(2,1)S(1)} fusion(bf16[3,2,2,2,1,12,96]{6,3,5,4,2,1,0:T(2,128)(2,1)} %param.5, pred[12,96]{1,0:T(8,128)(4,1)S(1)} %iota_compare_fusion.1), kind=kLoop, calls=%fused_computation.19 | loop fusion | flops 27648 | bytes 111744 | tf_op jit(solution)/shard_map/reshape.5
  8.3 0.9 %fusion.1 = bf16[96,3,2,2,2,1,12]{0,6,4,3,2,1,5:T(8,128)(2,1)S(1)} fusion(bf16[3,2,2,2,12,96]{5,3,4,2,1,0:T(2,128)(2,1)S(1)} %fusion.9, s32[96]{0:T(128)} %param.8), kind=kOutput, calls=%fused_computation.3 | convolution fusion | flops 5345280 | bytes 110976 | tf_op jit(solution)/shard_map/dot_general | solution.py:16
  9.2 0.7 %copy.19 = bf16[96,3,2,2,2,1,12]{6,4,3,2,1,5,0:T(2,128)(2,1)S(1)} copy(bf16[96,3,2,2,2,1,12]{0,6,4,3,2,1,5:T(8,128)(2,1)S(1)} %fusion.1) | data formatting | bytes 110592 | tf_op jit(solution)/shard_map/convert_element_type | solution.py:18
  9.8 1.7 %reshape.95 = bf16[4,2,3456]{2,1,0:T(2,128)(2,1)} reshape(bf16[96,1,3,2,2,2,12]{6,5,4,3,2,1,0:T(2,128)(2,1)S(1)} %bitcast.37) | data formatting | bytes 110592
  11.5 6.3 %all-to-all-start = ((bf16[4,2,3456]{2,1,0:T(2,128)(2,1)}), bf16[4,2,3456]{2,1,0:T(2,128)(2,1)S(1)}, u32[]{:S(2)}, u32[]{:S(2)}) async-start(bf16[4,2,3456]{2,1,0:T(2,128)(2,1)} %reshape.95), calls=%async_computation | async-start | bytes 110592 | tf_op jit(solution)/shard_map/all_to_all | solution.py:19
  17.9 0.0 reduce-scatter.2.cloned.1.call-start
  17.9 0.0 copy-done.2
  17.9 0.1 dynamic_slice.3
  17.9 5.6 %all-to-all-done = bf16[4,2,3456]{2,1,0:T(2,128)(2,1)S(1)} async-done(((bf16[4,2,3456]{2,1,0:T(2,128)(2,1)}), bf16[4,2,3456]{2,1,0:T(2,128)(2,1)S(1)}, u32[]{:S(2)}, u32[]{:S(2)}) %all-to-all-start) | async-done | bytes 55328 | tf_op jit(solution)/shard_map/all_to_all | solution.py:19
  23.6 1.4 %reshape.96 = bf16[96,1,3,2,2,2,12]{6,5,4,3,2,1,0:T(2,128)(2,1)S(1)} reshape(bf16[4,2,3456]{2,1,0:T(2,128)(2,1)S(1)} %all-to-all-done) | data formatting | bytes 110592
  25.0 1.0 %copy.32 = bf16[4,24,3,2,2,2,1,12]{1,0,5,7,4,3,2,6:T(4,128)(2,1)S(1)} copy(bf16[4,24,3,2,2,2,1,12]{7,5,4,3,2,1,0,6:T(2,128)(2,1)S(1)} %bitcast.38) | data formatting | bytes 110592 | tf_op jit(solution)/shard_map/all_to_all | solution.py:19
  26.0 0.0 copy-start.1
  26.0 0.2 copy.21
  26.2 0.2 copy.22
  26.4 7.6 %all_gather.3 = bf16[24,3,8,2,2,1,48]{6,0,5,4,3,1,2:T(8,128)(2,1)S(1)} all-gather(bf16[24,3,2,2,2,1,48]{6,0,5,4,3,1,2:T(8,128)(2,1)S(1)} %copy.22), channel_id=1, replica_groups=mesh['band'=4,'lev'=4,'grp'=2] {'lev'}, dimensions={2}, use_global_device_ids=true | all-gather | bytes 276480 | tf_op jit(solution)/shard_map/all_gather | solution.py:20
  34.0 0.2 copy_dynamic-update-slice_fusion
  34.2 0.0 copy-done.1
  34.2 0.3 fusion
  34.6 0.2 fusion.2
  34.8 0.0 copy-done
  34.8 0.4 fusion.4
  35.2 2.1 %copy.27 = f32[24,2,4,8,2,12]{0,3,4,2,1,5:T(8,128)} copy(f32[24,2,4,8,2,12]{5,3,4,2,1,0:T(8,128)S(1)} %fusion.4) | data formatting | bytes 294912 | tf_op jit(solution)/shard_map/dot_general | solution.py:38
  37.3 0.0 reduce-scatter.2.cloned.1.call-update
  37.3 0.1 broadcast_add_fusion
  37.4 15.2 %reduce-scatter.2.cloned.1.call-done = f32[24,2,4,8,2,6]{0,3,4,2,1,5:T(8,128)} async-done(((f32[24,2,4,8,2,12]{0,3,4,2,1,5:T(8,128)}), f32[24,2,4,8,2,6]{0,3,4,2,1,5:T(8,128)}) %reduce-scatter.2.cloned.1.call-update) | async-done | bytes 73744 | tf_op jit(solution)/shard_map/reduce_scatter | solution.py:41
  52.6 1.0 %select_convert_fusion = bf16[24,2,4,8,2,6]{0,3,4,2,1,5:T(8,128)(2,1)S(1)} fusion(f32[24,2,4,8,2,6]{0,3,4,2,1,5:T(8,128)} %reduce-scatter.2.cloned.1.call-done, pred[24,2,6]{0,1,2:T(4,128)(4,1)S(1)} %add_compare_fusion), kind=kLoop, calls=%fused_computation.13 | loop fusion | flops 18432 | bytes 110880 | tf_op jit(solution)/shard_map/convert_element_type | solution.py:54
  53.6 0.8 %copy.28 = bf16[24,2,4,8,2,6]{0,4,5,3,2,1:T(2,128)(2,1)} copy(bf16[24,2,4,8,2,6]{0,3,4,2,1,5:T(8,128)(2,1)S(1)} %select_convert_fusion) | data formatting | bytes 73728 | tf_op jit(solution)/shard_map/convert_element_type | solution.py:54
  (4 shorter events, 0.1 us)
Async XLA Ops:
  6.5 28.3 %copy-start = (bf16[24,2,12,1,48]{4,1,3,2,0:T(2,128)(2,1)S(1)}, bf16[24,2,12,1,48]{4,1,3,2,0:T(2,128)(2,1)}, u32[]{:S(2)}) copy-start(bf16[24,2,12,1,48]{4,1,3,2,0:T(2,128)(2,1)} %param.6) | copy-start | bytes 165892
  6.5 11.3 %copy-start.2 = (s32[96]{0:T(128)S(1)}, s32[96]{0:T(128)}, u32[]{:S(2)}) copy-start(s32[96]{0:T(128)} %param.8) | copy-start | bytes 1156
  11.5 12.1 %all-to-all-start = ((bf16[4,2,3456]{2,1,0:T(2,128)(2,1)}), bf16[4,2,3456]{2,1,0:T(2,128)(2,1)S(1)}, u32[]{:S(2)}, u32[]{:S(2)}) async-start(bf16[4,2,3456]{2,1,0:T(2,128)(2,1)} %reshape.95), calls=%async_computation | async-start | bytes 110592 | tf_op jit(solution)/shard_map/all_to_all | solution.py:19
  17.9 34.7 %reduce-scatter.2.cloned.1.call-start = ((), (), s32[]{:S(2)}) async-start(), calls=%async_computation.2 | async-start | bytes 1179648 | tf_op jit(solution)/shard_map/reduce_scatter | solution.py:41
  26.0 8.2 %copy-start.1 = (f32[8,8]{1,0:T(8,128)S(1)}, f32[8,8]{1,0:T(8,128)}, u32[]{:S(2)}) copy-start(f32[8,8]{1,0:T(8,128)} %param.9) | copy-start | bytes 772
Sparse Core Ops, SparseCore 0:
  37.4 15.1 reduce-scatter.1
where the time goes:
time: 61.6 us; the launch traced here: 61.3 us
  waiting for transfers between devices  20.9 us (34%)
  between operations  13.5 us (22%)
  local copies, waits for them, and re-layouts  8.37 us (14%)
  blocking collectives  7.56 us (12%)
  starting transfers between devices  6.35 us (10%)
  other arithmetic  3.09 us (5%)
  matrix products  1.56 us (3%)
    reduce_scatter x1, waiting for transfers between devices, body(): lax.psum_scatter(partial_value, 'grp', scatter_dimension=5, tiled=True)  15.2 us
    all_gather x1, blocking collectives, body(): coeffs = lax.all_gather(at_owners, 'lev', axis=2, tiled=True)  7.56 us
    all_to_all x1, starting transfers between devices, body(): lax.all_to_all(ordered, 'band', split_axis=0, concat_axis=6, tiled=True)  6.35 us
    all_to_all x1, waiting for transfers between devices, body(): lax.all_to_all(ordered, 'band', split_axis=0, concat_axis=6, tiled=True)  5.63 us
    unnamed x9, local copies, waits for them, and re-layouts  3.28 us
    dot_general x1, local copies, waits for them, and re-layouts, body(): lax.dot_general(parity, legendre, (((5, 6), (3, 4)), ((0, 4), (0, 1))), p...  2.07 us
    all_to_all x3, local copies, waits for them, and re-layouts, body(): lax.all_to_all(ordered, 'band', split_axis=0, concat_axis=6, tiled=True)  1.41 us
  transfers between devices with their start and end apart: 2, of which 2 were waited for; matrix products, arithmetic and copies ran while one was open for 0% of the time, Pallas kernels for 0%

commit v1 on v0

--- a/solution.py
+++ b/solution.py
@@ -2,6 +2,17 @@
 import jax.numpy as jnp
 from jax import lax
 from jax.sharding import PartitionSpec as P
+
+
+def ring_gather(value, axis, dim):
+    ways = lax.axis_size(axis)
+    pieces = [value]
+    for far in range(1, ways):
+        pieces.append(
+            lax.ppermute(pieces[far - 1], axis, [(d, (d - 1) % ways) for d in range(ways)])
+        )
+    line = jnp.concatenate(pieces, axis=dim)
+    return jnp.roll(line, lax.axis_index(axis) * value.shape[dim], axis=dim)
 
 
 def body(fourier, legendre, lat_points, wave_slots, vertical):
@@ -17,7 +28,7 @@
         slot_table, masked, (((1,), (6,)), ((), ())), preferred_element_type=jnp.float32
     ).astype(jnp.bfloat16)
     at_owners = lax.all_to_all(ordered, "band", split_axis=0, concat_axis=6, tiled=True)
-    coeffs = lax.all_gather(at_owners, "lev", axis=2, tiled=True)
+    coeffs = ring_gather(at_owners, "lev", 2)
     level_count = coeffs.shape[2]
     level_rows = lax.broadcasted_iota(jnp.int32, (level_count, level_count), 0)
     level_cols = lax.broadcasted_iota(jnp.int32, (level_count, level_count), 1)

time: 61.6 us -> 69.1 us (1.12)
  blocking collectives: 7.56 us -> 11.9 us
  waiting for transfers between devices: 20.9 us -> 24.5 us
  starting transfers between devices: 6.35 us -> 3.84 us
  local copies, waits for them, and re-layouts: 8.37 us -> 10.5 us
    all_to_all x0 -> x1, blocking collectives: none -> 11.9 us  [body(): lax.all_to_all(ordered, 'band', split_axis=0, concat_axis=6, tiled=True)]
    ppermute x0 -> x3, waiting for transfers between devices: none -> 7.94 us  [ring_gather(): lax.ppermute(pieces[far - 1], axis, [(d, (d - 1) % ways) for d in range(w...]
    all_gather x1 -> x0, blocking collectives: 7.56 us -> none  [body(): coeffs = lax.all_gather(at_owners, 'lev', axis=2, tiled=True)]
    all_to_all x1 -> x0, starting transfers between devices: 6.35 us -> none  [body(): lax.all_to_all(ordered, 'band', split_axis=0, concat_axis=6, tiled=True)]
    all_to_all x1 -> x0, waiting for transfers between devices: 5.63 us -> none  [body(): lax.all_to_all(ordered, 'band', split_axis=0, concat_axis=6, tiled=True)]
    ppermute x0 -> x3, starting transfers between devices: none -> 3.84 us  [ring_gather(): lax.ppermute(pieces[far - 1], axis, [(d, (d - 1) % ways) for d in range(w...]
    concatenate x1, local copies, waits for them, and re-layouts: 0.04 us -> 2.14 us  [ring_gather(): return jnp.roll(line, lax.axis_index(axis) * value.shape[dim], axis=dim)]
    reduce_scatter x1, waiting for transfers between devices: 15.2 us -> 16.6 us  [body(): lax.psum_scatter(partial_value, 'grp', scatter_dimension=5, tiled=True)]
  transfers between devices with their start and end apart: 2 -> 4, of which waited for: 2 -> 4; matrix products, arithmetic and copies ran while one was open for 0% -> 0% of each run, Pallas kernels for 0% -> 0%
where the time goes in v1:
time: 69.1 us; the launch traced here: 68.8 us
  waiting for transfers between devices  24.5 us (35%)
  between operations  13.5 us (20%)
  blocking collectives  11.9 us (17%)
  local copies, waits for them, and re-layouts  10.5 us (15%)
  starting transfers between devices  3.84 us (6%)
  other arithmetic  3.06 us (4%)
  matrix products  1.56 us (2%)
    reduce_scatter x1, waiting for transfers between devices, body(): lax.psum_scatter(partial_value, 'grp', scatter_dimension=5, tiled=True)  16.6 us
    all_to_all x1, blocking collectives, body(): lax.all_to_all(ordered, 'band', split_axis=0, concat_axis=6, tiled=True)  11.9 us
    ppermute x3, waiting for transfers between devices, ring_gather(): lax.ppermute(pieces[far - 1], axis, [(d, (d - 1) % ways) for d in range(w...  7.94 us
    ppermute x3, starting transfers between devices, ring_gather(): lax.ppermute(pieces[far - 1], axis, [(d, (d - 1) % ways) for d in range(w...  3.84 us
    unnamed x8, local copies, waits for them, and re-layouts  2.9 us
    concatenate x1, local copies, waits for them, and re-layouts, ring_gather(): return jnp.roll(line, lax.axis_index(axis) * value.shape[dim], axis=dim)  2.14 us
    dot_general x1, local copies, waits for them, and re-layouts, body(): lax.dot_general(parity, legendre, (((5, 6), (3, 4)), ((0, 4), (0, 1))), p...  2.06 us
    all_to_all x3, local copies, waits for them, and re-layouts, body(): lax.all_to_all(ordered, 'band', split_axis=0, concat_axis=6, tiled=True)  1.61 us
  transfers between devices with their start and end apart: 4, of which 4 were waited for; matrix products, arithmetic and copies ran while one was open for 0% of the time, Pallas kernels for 0%

profile of v1, /device:TPU:0, one launch (start us, length us, event | category | flops | bytes accessed | tf_op | source)
XLA Modules:
  0.0 68.8 jit_solution(11029262747874184629)
XLA Ops:
  6.5 0.7 %minimum_bitcast_fusion = s32[12]{0:T(128)S(1)} fusion(s32[1,12]{1,0:T(1,128)} %param.7), kind=kLoop, calls=%fused_computation.35 | loop fusion | flops 204 | bytes 96 | tf_op jit(solution)/shard_map/le | solution.py:22
  7.2 0.1 iota_compare_fusion.1
  7.3 1.0 %fusion.9 = bf16[3,2,2,2,12,96]{5,3,4,2,1,0:T(2,128)(2,1)S(1)} fusion(bf16[3,2,2,2,1,12,96]{6,3,5,4,2,1,0:T(2,128)(2,1)} %param.5, pred[12,96]{1,0:T(8,128)(4,1)S(1)} %iota_compare_fusion.1), kind=kLoop, calls=%fused_computation.20 | loop fusion | flops 27648 | bytes 111744 | tf_op jit(solution)/shard_map/reshape.5
  8.3 0.9 %fusion.1 = bf16[96,3,2,2,2,1,12]{0,6,4,3,2,1,5:T(8,128)(2,1)S(1)} fusion(bf16[3,2,2,2,12,96]{5,3,4,2,1,0:T(2,128)(2,1)S(1)} %fusion.9, s32[96]{0:T(128)} %param.8), kind=kOutput, calls=%fused_computation.3 | convolution fusion | flops 5345280 | bytes 110976 | tf_op jit(solution)/shard_map/dot_general | solution.py:27
  9.2 0.7 copy.21
  9.8 1.0 %reshape.95 = bf16[4,2,3456]{2,1,0:T(2,128)(2,1)S(1)} reshape(bf16[96,1,3,2,2,2,12]{6,5,4,3,2,1,0:T(2,128)(2,1)S(1)} %bitcast.38) | data formatting | bytes 110592
  10.9 11.9 %all_to_all.18 = bf16[4,2,3456]{2,1,0:T(2,128)(2,1)S(1)} all-to-all(bf16[4,2,3456]{2,1,0:T(2,128)(2,1)S(1)} %reshape.95), channel_id=1, replica_groups=mesh['band'=4,'lev'=4,'grp'=2] {'band'}, dimensions={0} | all-to-all | bytes 110592 | tf_op jit(solution)/shard_map/all_to_all | solution.py:30
  22.8 1.4 %reshape.96 = bf16[96,1,3,2,2,2,12]{6,5,4,3,2,1,0:T(2,128)(2,1)S(1)} reshape(bf16[4,2,3456]{2,1,0:T(2,128)(2,1)S(1)} %all_to_all.18) | data formatting | bytes 110592
  24.1 1.0 %copy.34 = bf16[4,24,3,2,2,2,1,12]{1,0,5,7,4,3,2,6:T(4,128)(2,1)S(1)} copy(bf16[4,24,3,2,2,2,1,12]{7,5,4,3,2,1,0,6:T(2,128)(2,1)S(1)} %bitcast.39) | data formatting | bytes 110592 | tf_op jit(solution)/shard_map/all_to_all | solution.py:30
  25.2 0.2 copy.23
  25.4 0.4 copy.25
  25.8 0.1 collective-permute-start
  25.8 2.7 %collective-permute-done = bf16[24,3,2,2,2,1,48]{6,2,4,3,0,5,1:T(2,128)(2,1)S(1)} collective-permute-done((bf16[24,3,2,2,2,1,48]{6,2,4,3,0,5,1:T(2,128)(2,1)S(1)}, bf16[24,3,2,2,2,1,48]{6,2,4,3,0,5,1:T(2,128)(2,1)S(1)}, u32[]{:S(2)}, u32[]{:S(2)}) %collective-permute-start) | collective-permute-done | bytes 55328 | tf_op jit(solution)/shard_map/ppermute | solution.py:12
  28.5 1.9 %collective-permute-start.1 = (bf16[24,3,2,2,2,1,48]{6,2,4,3,0,5,1:T(2,128)(2,1)S(1)}, bf16[24,3,2,2,2,1,48]{6,2,4,3,0,5,1:T(2,128)(2,1)S(1)}, u32[]{:S(2)}, u32[]{:S(2)}) collective-permute-start(bf16[24,3,2,2,2,1,48]{6,2,4,3,0,5,1:T(2,128)(2,1)S(1)} %collective-permute-done), channel_id=1, source_target_pairs={{0,6},{2,0},{4,2},{6,4},{1,7},{3,1},{5,3},{7,5},{8,14},{10,8},{12,... | collective-permute-start | bytes 165896 | tf_op jit(solution)/shard_map/ppermute | solution.py:12
  30.4 2.7 %collective-permute-done.1 = bf16[24,3,2,2,2,1,48]{6,2,4,3,0,5,1:T(2,128)(2,1)S(1)} collective-permute-done((bf16[24,3,2,2,2,1,48]{6,2,4,3,0,5,1:T(2,128)(2,1)S(1)}, bf16[24,3,2,2,2,1,48]{6,2,4,3,0,5,1:T(2,128)(2,1)S(1)}, u32[]{:S(2)}, u32[]{:S(2)}) %collective-permute-start.1) | collective-permute-done | bytes 55328 | tf_op jit(solution)/shard_map/ppermute | solution.py:12
  33.1 1.9 %collective-permute-start.2 = (bf16[24,3,2,2,2,1,48]{6,2,4,3,0,5,1:T(2,128)(2,1)S(1)}, bf16[24,3,2,2,2,1,48]{6,2,4,3,0,5,1:T(2,128)(2,1)S(1)}, u32[]{:S(2)}, u32[]{:S(2)}) collective-permute-start(bf16[24,3,2,2,2,1,48]{6,2,4,3,0,5,1:T(2,128)(2,1)S(1)} %collective-permute-done.1), channel_id=1, source_target_pairs={{0,6},{2,0},{4,2},{6,4},{1,7},{3,1},{5,3},{7,5},{8,14},{10,8},{12,... | collective-permute-start | bytes 165896 | tf_op jit(solution)/shard_map/ppermute | solution.py:12
  35.0 0.1 dynamic_slice.7
  35.0 2.6 %collective-permute-done.2 = bf16[24,3,2,2,2,1,48]{6,2,4,3,0,5,1:T(2,128)(2,1)S(1)} collective-permute-done((bf16[24,3,2,2,2,1,48]{6,2,4,3,0,5,1:T(2,128)(2,1)S(1)}, bf16[24,3,2,2,2,1,48]{6,2,4,3,0,5,1:T(2,128)(2,1)S(1)}, u32[]{:S(2)}, u32[]{:S(2)}) %collective-permute-start.2) | collective-permute-done | bytes 55328 | tf_op jit(solution)/shard_map/ppermute | solution.py:12
  37.6 2.1 %concatenate.9 = bf16[24,3,16,2,2,1,48]{6,2,4,3,0,5,1:T(8,128)(2,1)S(1)} concatenate(bf16[24,3,2,2,2,1,48]{6,2,4,3,0,5,1:T(2,128)(2,1)S(1)} %copy.25, bf16[24,3,2,2,2,1,48]{6,2,4,3,0,5,1:T(2,128)(2,1)S(1)} %collective-permute-done, bf16[24,3,2,2,2,1,48]{6,2,4,3,0,5,1:T(2,128)(2,1)S(1)} %collective-permute-done.1, bf16[24,3,2,2,2,1,48]{6,2,4,3,0,5,1:T(2,128)(2,1)S(1)} %collective-permute-done.2, ...), dimensions={2} | concatenate | bytes 884736 | tf_op jit(solution)/shard_map/jit(_roll_dynamic)/concatenate | solution.py:15
  39.8 0.0 copy-start.1
  39.8 0.2 constant_dynamic-slice_fusion
  40.0 0.5 copy-done.1
  40.5 0.3 fusion
  40.8 0.2 fusion.2
  41.0 0.0 copy-done
  41.0 0.4 fusion.4
  41.4 2.1 %copy.29 = f32[24,2,4,8,2,12]{0,3,4,2,1,5:T(8,128)} copy(f32[24,2,4,8,2,12]{5,3,4,2,1,0:T(8,128)S(1)} %fusion.4) | data formatting | bytes 294912 | tf_op jit(solution)/shard_map/dot_general | solution.py:49
  43.4 0.0 reduce-scatter.2.cloned.1.call-update
  43.5 0.1 broadcast_add_fusion
  43.5 16.6 %reduce-scatter.2.cloned.1.call-done = f32[24,2,4,8,2,6]{0,3,4,2,1,5:T(8,128)} async-done(((f32[24,2,4,8,2,12]{0,3,4,2,1,5:T(8,128)}), f32[24,2,4,8,2,6]{0,3,4,2,1,5:T(8,128)}) %reduce-scatter.2.cloned.1.call-update) | async-done | bytes 73744 | tf_op jit(solution)/shard_map/reduce_scatter | solution.py:52
  60.1 1.0 %select_convert_fusion = bf16[24,2,4,8,2,6]{0,3,4,2,1,5:T(8,128)(2,1)S(1)} fusion(f32[24,2,4,8,2,6]{0,3,4,2,1,5:T(8,128)} %reduce-scatter.2.cloned.1.call-done, pred[24,2,6]{0,1,2:T(4,128)(4,1)S(1)} %add_compare_fusion), kind=kLoop, calls=%fused_computation.15 | loop fusion | flops 18432 | bytes 110880 | tf_op jit(solution)/shard_map/convert_element_type | solution.py:65
  61.2 0.8 %copy.30 = bf16[24,2,4,8,2,6]{0,4,5,3,2,1:T(2,128)(2,1)} copy(bf16[24,2,4,8,2,6]{0,3,4,2,1,5:T(8,128)(2,1)S(1)} %select_convert_fusion) | data formatting | bytes 73728 | tf_op jit(solution)/shard_map/convert_element_type | solution.py:65
  (6 shorter events, 0.0 us)
Async XLA Ops:
  6.5 34.5 %copy-start = (bf16[24,2,12,1,48]{4,1,3,2,0:T(2,128)(2,1)S(1)}, bf16[24,2,12,1,48]{4,1,3,2,0:T(2,128)(2,1)}, u32[]{:S(2)}) copy-start(bf16[24,2,12,1,48]{4,1,3,2,0:T(2,128)(2,1)} %param.6) | copy-start | bytes 165892
  6.5 53.6 %reduce-scatter.2.cloned.1.call-start = ((), (), s32[]{:S(2)}) async-start(), calls=%async_computation.2 | async-start | bytes 1179648 | tf_op jit(solution)/shard_map/reduce_scatter | solution.py:52
  22.7 12.2 %copy-start.2 = (s32[96]{0:T(128)S(1)}, s32[96]{0:T(128)}, u32[]{:S(2)}) copy-start(s32[96]{0:T(128)} %param.8) | copy-start | bytes 1156
  25.8 2.7 %collective-permute-start = (bf16[24,3,2,2,2,1,48]{6,2,4,3,0,5,1:T(2,128)(2,1)S(1)}, bf16[24,3,2,2,2,1,48]{6,2,4,3,0,5,1:T(2,128)(2,1)S(1)}, u32[]{:S(2)}, u32[]{:S(2)}) collective-permute-start(bf16[24,3,2,2,2,1,48]{6,2,4,3,0,5,1:T(2,128)(2,1)S(1)} %copy.25), channel_id=1, source_target_pairs={{0,6},{2,0},{4,2},{6,4},{1,7},{3,1},{5,3},{7,5},{8,14},{10,8},{12,... | collective-permute-start | bytes 165896 | tf_op jit(solution)/shard_map/ppermute | solution.py:12
  28.5 4.6 %collective-permute-start.1 = (bf16[24,3,2,2,2,1,48]{6,2,4,3,0,5,1:T(2,128)(2,1)S(1)}, bf16[24,3,2,2,2,1,48]{6,2,4,3,0,5,1:T(2,128)(2,1)S(1)}, u32[]{:S(2)}, u32[]{:S(2)}) collective-permute-start(bf16[24,3,2,2,2,1,48]{6,2,4,3,0,5,1:T(2,128)(2,1)S(1)} %collective-permute-done), channel_id=1, source_target_pairs={{0,6},{2,0},{4,2},{6,4},{1,7},{3,1},{5,3},{7,5},{8,14},{10,8},{12,... | collective-permute-start | bytes 165896 | tf_op jit(solution)/shard_map/ppermute | solution.py:12
  33.1 4.6 %collective-permute-start.2 = (bf16[24,3,2,2,2,1,48]{6,2,4,3,0,5,1:T(2,128)(2,1)S(1)}, bf16[24,3,2,2,2,1,48]{6,2,4,3,0,5,1:T(2,128)(2,1)S(1)}, u32[]{:S(2)}, u32[]{:S(2)}) collective-permute-start(bf16[24,3,2,2,2,1,48]{6,2,4,3,0,5,1:T(2,128)(2,1)S(1)} %collective-permute-done.1), channel_id=1, source_target_pairs={{0,6},{2,0},{4,2},{6,4},{1,7},{3,1},{5,3},{7,5},{8,14},{10,8},{12,... | collective-permute-start | bytes 165896 | tf_op jit(solution)/shard_map/ppermute | solution.py:12
  39.8 0.7 %copy-start.1 = (f32[8,8]{1,0:T(8,128)S(1)}, f32[8,8]{1,0:T(8,128)}, u32[]{:S(2)}) copy-start(f32[8,8]{1,0:T(8,128)} %param.9) | copy-start | bytes 772
Sparse Core Ops, SparseCore 0:
  43.6 16.4 reduce-scatter.1
